TPU v7x, 512 devices: a whole 4x8x8 slice. The times are simulated.
512 devices in a mesh: seq: 16 (over y_hi, z), head: 32 (over x, y_lo, core).
Axes of the slice: x: 4, y: 8 (y_hi: 2, y_lo: 4; y = y_hi * 4 + y_lo), z: 8, core: 2. Of those that a mesh axis runs over, the one named last changes fastest.
Arguments:
- tokens: bfloat16 [16384, 4096], P(('seq', 'head')), may hold values from -6 to 6
- doc_lengths: int32 [16], replicated, may hold values from 1 to 8704, as said below
- value_weight: bfloat16 [4096, 8192], P('seq', 'head'), may hold values from -0.09375 to 0.09375
- gate_weight: bfloat16 [4096, 8192], P('seq', 'head'), may hold values from -0.09375 to 0.09375
- state_weight: bfloat16 [8, 4096, 256], P(None, 'seq'), may hold values from -0.09375 to 0.09375
- step_weight: bfloat16 [4096, 128], P('seq', 'head'), may hold values from -0.09375 to 0.09375
- value_conv: float32 [4, 8192], P(None, 'head'), may hold values from -3 to 3
- state_conv: float32 [8, 4, 256], replicated, may hold values from -3 to 3
- step_bias: float32 [128], P('head'), may hold values from -5 to -3
- log_rate: float32 [128], P('head'), may hold values from -6 to 4
Outputs:
- layer_output: bfloat16 [16384, 8192], P('seq', 'head')
Inputs may be any that keep to these rules, and one draw needn't show every extreme that they name: `doc_lengths`: the 16 documents lie one after another, their lengths sum to 16384, and the last one holds 8704 positions.
All inputs are finite; a program needn't handle non-finite values.
Results may differ from a plain program's by a relative error of at most 0.015.
Values may be sent and summed in bfloat16 or wider, within the bound.
No kernel may reach another device: no remote copies, remote signals or barrier semaphores. Data moves between devices by JAX's collectives and lax.ppermute only.
A program may use at most 64 MiB of HBM per device.

v0:
```python
import jax
import jax.numpy as jnp
from jax import lax
from jax.sharding import Mesh
from jax.sharding import PartitionSpec as P

HEADS = 128
GROUPS = 8
BLOCK = 256
STATE = 128
YH, Z, X, Y, C = (2, 8, 4, 4, 2)
SEQ = ("yh", "z")
HEAD = ("x", "y", "c")
F32 = jnp.float32
BF16 = jnp.bfloat16


def ring(count, step):
    return [(i, (i + step) % count) for i in range(count)]


def along_seq(value, step):
    return lax.ppermute(value, SEQ, [(i, i + step) for i in range(YH * Z - step)])


def ring_gather(block):
    half = block.shape[1] // 2
    right = left = block
    z = lax.axis_index("z")
    held = jnp.zeros((Z,) + block.shape, block.dtype)

    def put(held, piece, offset, row):
        return lax.dynamic_update_slice(held, piece[None], ((z + offset) % Z, 0, row, 0))

    held = put(held, block, 0, 0)
    for step in range(1, 4):
        right = lax.ppermute(right, "z", ring(Z, 1))
        left = lax.ppermute(left, "z", ring(Z, -1))
        held = put(held, right, -step + Z, 0)
        held = put(held, left, step, 0)
    right = lax.ppermute(right[:, :half], "z", ring(Z, 1))
    left = lax.ppermute(left[:, half:], "z", ring(Z, -1))
    held = put(held, right, 4, 0)
    held = put(held, left, 4, half)
    return held


def segment_of(positions, starts):
    reached = (starts[None, :] <= positions[:, None]).astype(jnp.int32)
    return jnp.sum(reached, axis=1) - 1


def causal_conv(extended, taps_weight, seg_ext, row_count):
    tap_count = taps_weight.shape[0]
    own_segment = seg_ext[tap_count - 1 :]
    summed = jnp.zeros((row_count, extended.shape[1]), F32)
    for tap_index in range(tap_count):
        window = extended[tap_index : tap_index + row_count].astype(F32)
        keep_mask = (seg_ext[tap_index : tap_index + row_count] == own_segment).astype(F32)
        summed = summed + taps_weight[tap_index][None, :] * window * keep_mask[:, None]
    return jax.nn.silu(summed).astype(BF16)


def block_terms(b_rows, c_rows, x_rows, decay_rows, step_rows, segments, seg_before):
    block_len = b_rows.shape[0]
    head_total = decay_rows.shape[0]
    x_heads = x_rows.reshape(block_len, head_total, -1)
    cumulative = jnp.cumsum(decay_rows, axis=1)
    products = jnp.dot(c_rows, b_rows.T, preferred_element_type=F32)
    local_index = jnp.arange(block_len)
    allowed = (local_index[None, :] <= local_index[:, None]) & (
        segments[None, :] == segments[:, None]
    )
    spread = cumulative[:, :, None] - cumulative[:, None, :]
    decay_mat = jnp.where(allowed[None], jnp.exp(jnp.where(allowed[None], spread, 0.0)), 0.0)
    scores = (products[None] * decay_mat * step_rows[:, None, :]).astype(BF16)
    y_inner = jnp.einsum("hij,jhp->ihp", scores, x_heads, preferred_element_type=F32)
    ending = cumulative[:, -1]
    trailing = (
        jnp.where((segments == segments[-1])[None, :], jnp.exp(ending[:, None] - cumulative), 0.0)
        * step_rows
    )
    weighted = (trailing.T[:, :, None] * x_heads.astype(F32)).astype(BF16)
    local_state = jnp.dot(b_rows.T, weighted.reshape(block_len, -1), preferred_element_type=F32)
    factor = jnp.where(segments[-1] == seg_before, jnp.exp(ending), 0.0)
    entry_gain = jnp.where((segments == seg_before)[None, :], jnp.exp(cumulative), 0.0)
    return (y_inner.reshape(block_len, -1), local_state, factor, entry_gain)


def spread_heads(values, width):
    return jnp.repeat(values, width, axis=-1)


def scan_shards(state, gain):
    rows = jnp.broadcast_to(gain[None, :], (8, gain.shape[0]))
    packed = jnp.concatenate([state, rows], axis=0)
    near = [along_seq(packed, step) for step in (1, 2, 3)]
    total, gains = (packed[:STATE], packed[STATE : STATE + 1])
    for piece in near:
        total = total + gains * piece[:STATE]
        gains = gains * piece[STATE : STATE + 1]
    packed = jnp.concatenate([total, jnp.broadcast_to(gains, (8, gains.shape[1]))], axis=0)
    first, second = (along_seq(packed, 1), along_seq(packed, 5))
    return first[:STATE] + first[STATE : STATE + 1] * second[:STATE]


def local(
    tokens,
    doc_lengths,
    value_weight,
    gate_weight,
    state_weight,
    step_weight,
    value_conv,
    state_conv,
    step_bias,
    log_rate,
):
    tok_dev = tokens.shape[0] * X * Y * C
    heads_here = step_weight.shape[1]
    tap_count = value_conv.shape[0]
    blocks = tok_dev // BLOCK
    cols = value_weight.shape[1]
    core = lax.axis_index("c")
    group = lax.axis_index("x") * 2 + lax.axis_index("y") // 2
    gathered = lax.all_gather(tokens, HEAD, axis=0, tiled=True)
    state_own = lax.dynamic_index_in_dim(state_weight, group, 0, keepdims=False)
    conv_own = lax.dynamic_index_in_dim(state_conv, group, 0, keepdims=False)
    state_half = jnp.where(core == 0, state_own[:, :STATE], state_own[:, STATE:])
    state_half = jnp.concatenate([state_half[:STATE], state_half[STATE:]], axis=1)
    step_rows = jnp.pad(step_weight.T, ((0, 8 - heads_here), (0, 0)))
    pack = jnp.concatenate([value_weight, state_half, step_rows, gate_weight], axis=0)
    both = lax.all_gather(pack, "yh", axis=0, tiled=False)
    first_rows = 256 + STATE + 8
    gate_all = lax.all_gather(both[:, first_rows:], "z", axis=0, tiled=False)
    held = ring_gather(both[:, :first_rows]).transpose(1, 0, 2, 3)
    depth = tokens.shape[1]
    value_all = held[:, :, :256].reshape(depth, cols)
    state_all = held[:, :, 256 : 256 + STATE]
    state_all = jnp.stack([state_all[..., :STATE], state_all[..., STATE:]], axis=2)
    state_all = state_all.reshape(depth, STATE)
    step_all = held[:, :, 256 + STATE :].transpose(0, 1, 3, 2).reshape(depth, 8)[:, :heads_here]
    half_proj = jnp.dot(gathered, state_all, preferred_element_type=F32).astype(BF16)
    other_proj = lax.ppermute(half_proj, "c", [(0, 1), (1, 0)])
    value_proj = jnp.dot(gathered, value_all, preferred_element_type=F32).astype(BF16)
    step_proj = jnp.dot(gathered, step_all, preferred_element_type=F32).astype(BF16)
    b_proj = jnp.where(core == 0, half_proj, other_proj)
    c_proj = jnp.where(core == 0, other_proj, half_proj)
    state_proj = jnp.concatenate([b_proj, c_proj], axis=1)
    rim_source = jnp.concatenate(
        [value_proj[-(tap_count - 1) :], state_proj[-(tap_count - 1) :]], axis=1
    )
    rim_rows = along_seq(rim_source, 1)
    value_ext = jnp.concatenate([rim_rows[:, :cols], value_proj], axis=0)
    state_ext = jnp.concatenate([rim_rows[:, cols:], state_proj], axis=0)
    starts = jnp.cumsum(doc_lengths) - doc_lengths
    positions = lax.axis_index(SEQ) * tok_dev + jnp.arange(-(tap_count - 1), tok_dev)
    seg_ext = segment_of(positions, starts)
    value_act = causal_conv(value_ext, value_conv, seg_ext, tok_dev)
    state_act = causal_conv(state_ext, conv_own, seg_ext, tok_dev)
    step_size = jax.nn.softplus(step_proj.astype(F32) + step_bias[None, :])
    decay_rate = -jnp.exp(log_rate)[None, :] * step_size
    seg_rows = seg_ext[tap_count - 1 :].reshape(blocks, BLOCK)
    seg_before = seg_ext[tap_count - 2 : tap_count - 2 + tok_dev : BLOCK]
    b_all = state_act[:, :STATE].reshape(blocks, BLOCK, STATE)
    c_all = state_act[:, STATE:].reshape(blocks, BLOCK, STATE)
    x_all = value_act.reshape(blocks, BLOCK, cols)
    decay_all = decay_rate.reshape(blocks, BLOCK, heads_here).transpose(0, 2, 1)
    step_all = step_size.reshape(blocks, BLOCK, heads_here).transpose(0, 2, 1)
    y_inner, local_state, factor, entry_gain = lax.map(
        lambda item: block_terms(*item),
        (b_all, c_all, x_all, decay_all, step_all, seg_rows, seg_before),
    )
    width = cols // heads_here
    factor = spread_heads(factor, width)
    running = jnp.zeros((STATE, cols), F32)
    gain = jnp.ones((cols,), F32)
    inside, gains = ([], [])
    for index in range(blocks):
        inside.append(running)
        gains.append(gain)
        running = factor[index][None, :] * running + local_state[index]
        gain = gain * factor[index]
    entering = scan_shards(running, gain)
    gate_full = gate_all.transpose(1, 0, 2, 3).reshape(depth, cols)
    gate_proj = jnp.dot(gathered, gate_full, preferred_element_type=F32).astype(BF16)
    outs = []
    for index in range(blocks):
        incoming = inside[index] + gains[index][None, :] * entering
        carried = jnp.dot(c_all[index].astype(F32), incoming, precision=lax.Precision.HIGHEST)
        carried = carried * spread_heads(entry_gain[index].T, width)
        total = y_inner[index] + carried + x_all[index].astype(F32)
        gating = jax.nn.silu(gate_proj[index * BLOCK : (index + 1) * BLOCK].astype(F32))
        outs.append((total * gating).astype(BF16))
    return jnp.concatenate(outs, axis=0)


def solution(mesh):
    grid = Mesh(mesh.devices.reshape(YH, Z, X, Y, C), SEQ + HEAD)
    return jax.shard_map(
        local,
        mesh=grid,
        in_specs=(
            P(SEQ + HEAD, None),
            P(),
            P(SEQ, HEAD),
            P(SEQ, HEAD),
            P(None, SEQ, None),
            P(SEQ, HEAD),
            P(None, HEAD),
            P(),
            P(HEAD),
            P(HEAD),
        ),
        out_specs=P(SEQ, HEAD),
        check_vma=False,
    )
```

profile of v0, /device:TPU:112, one launch (start us, length us, event | category | flops | bytes accessed | tf_op | source)
XLA Modules:
  0.0 297.2 jit_solution(12818761446502483740)
XLA Ops:
  6.6 1.2 copy-done
  8.8 21.0 %all-gather = bf16[1296,256]{1,0:T(8,128)(2,1)S(1)} all-gather(bf16[648,256]{1,0:T(8,128)(2,1)S(1)} %fusion.47), channel_id=2, replica_groups=mesh['yh'=2,'z'=8,'x'=4,'y'=4,'c'=2] {'yh'}, dimensions={0}, use_global_device_ids=true | all-gather | bytes 995328 | tf_op jit(solution)/shard_map/all_gather | solution.py:133
  31.4 4.3 %collective-permute-start = (bf16[2,392,256]{2,1,0:T(8,128)(2,1)S(1)}, bf16[2,392,256]{2,1,0:T(8,128)(2,1)S(1)}, u32[]{:S(2)}, u32[]{:S(2)}) collective-permute-start(bf16[2,392,256]{2,1,0:T(8,128)(2,1)S(1)} %slice.371), channel_id=1, source_target_pairs={{0,32},{32,64},{64,96},{96,128},{128,160},{160,192},{192,224},{224... | collective-permute-start | bytes 1204232 | tf_op jit(solution)/shard_map/ppermute | solution.py:37
  35.6 1.9 collective-permute-start.1
  39.2 1.9 broadcast_in_dim.172
  42.0 1.4 collective-permute-done
  43.4 4.3 %collective-permute-start.2 = (bf16[2,392,256]{2,1,0:T(8,128)(2,1)S(1)}, bf16[2,392,256]{2,1,0:T(8,128)(2,1)S(1)}, u32[]{:S(2)}, u32[]{:S(2)}) collective-permute-start(bf16[2,392,256]{2,1,0:T(8,128)(2,1)S(1)} %collective-permute-done), channel_id=1, source_target_pairs={{0,32},{32,64},{64,96},{96,128},{128,160},{160,192},{192,224},{224... | collective-permute-start | bytes 1204232 | tf_op jit(solution)/shard_map/ppermute | solution.py:37
  48.1 8.5 %collective-permute-start.3 = (bf16[2,392,256]{2,1,0:T(8,128)(2,1)S(1)}, bf16[2,392,256]{2,1,0:T(8,128)(2,1)S(1)}, u32[]{:S(2)}, u32[]{:S(2)}) collective-permute-start(bf16[2,392,256]{2,1,0:T(8,128)(2,1)S(1)} %collective-permute-done.1), channel_id=1, source_target_pairs={{0,224},{32,0},{64,32},{96,64},{128,96},{160,128},{192,160},{224,1... | collective-permute-start | bytes 1204232 | tf_op jit(solution)/shard_map/ppermute | solution.py:38
  58.1 9.0 %collective-permute-done.2 = bf16[2,392,256]{2,1,0:T(8,128)(2,1)S(1)} collective-permute-done((bf16[2,392,256]{2,1,0:T(8,128)(2,1)S(1)}, bf16[2,392,256]{2,1,0:T(8,128)(2,1)S(1)}, u32[]{:S(2)}, u32[]{:S(2)}) %collective-permute-start.2) | collective-permute-done | bytes 401440 | tf_op jit(solution)/shard_map/ppermute | solution.py:37
  67.2 2.8 collective-permute-start.4
  69.9 1.3 collective-permute-done.3
  71.3 5.5 %collective-permute-start.5 = (bf16[2,392,256]{2,1,0:T(8,128)(2,1)S(1)}, bf16[2,392,256]{2,1,0:T(8,128)(2,1)S(1)}, u32[]{:S(2)}, u32[]{:S(2)}) collective-permute-start(bf16[2,392,256]{2,1,0:T(8,128)(2,1)S(1)} %collective-permute-done.3), channel_id=1, source_target_pairs={{0,224},{32,0},{64,32},{96,64},{128,96},{160,128},{192,160},{224,1... | collective-permute-start | bytes 1204232 | tf_op jit(solution)/shard_map/ppermute | solution.py:38
  78.4 10.5 %collective-permute-done.4 = bf16[2,392,256]{2,1,0:T(8,128)(2,1)S(1)} collective-permute-done((bf16[2,392,256]{2,1,0:T(8,128)(2,1)S(1)}, bf16[2,392,256]{2,1,0:T(8,128)(2,1)S(1)}, u32[]{:S(2)}, u32[]{:S(2)}) %collective-permute-start.4) | collective-permute-done | bytes 401440 | tf_op jit(solution)/shard_map/ppermute | solution.py:37
  88.8 1.9 collective-permute-start.6
  90.8 3.9 %collective-permute-start.7 = (bf16[2,196,256]{2,1,0:T(8,128)(2,1)S(1)}, bf16[2,196,256]{2,1,0:T(8,128)(2,1)S(1)}, u32[]{:S(2)}, u32[]{:S(2)}) collective-permute-start(bf16[2,196,256]{2,1,0:T(8,128)(2,1)S(1)} %slice.373), channel_id=1, source_target_pairs={{0,224},{32,0},{64,32},{96,64},{128,96},{160,128},{192,160},{224,1... | collective-permute-start | bytes 602120 | tf_op jit(solution)/shard_map/ppermute | solution.py:42
  96.8 2.1 dynamic_update_slice.50
  98.9 1.8 dynamic_update_slice.51
  100.8 3.1 %slice.374 = bf16[2,8,256,256]{3,2,1,0:T(8,128)(2,1)} slice(bf16[2,8,392,256]{3,2,1,0:T(8,128)(2,1)} %bitcast.36), slice={[0:2], [0:8], [0:256], [0:256]} | slice | bytes 4194304 | tf_op jit(solution)/shard_map/slice | solution.py:138
  104.7 1.3 slice_bitcast_fusion.1
  106.2 3.2 %copy.121 = bf16[2,8,256,256]{3,2,1,0:T(8,128)(2,1)} copy(bf16[2,8,256,256]{3,2,0,1:T(8,128)(2,1)} %bitcast.241) | data formatting | bytes 4194304 | tf_op jit(solution)/shard_map/transpose | solution.py:185
  109.5 49.4 %all-gather.5.cloned.1.call-done = bf16[1024,4096]{1,0:T(8,128)(2,1)} async-done(((bf16[32,4096]{1,0:T(8,128)(2,1)}), bf16[1024,4096]{1,0:T(8,128)(2,1)}) %all-gather.5.cloned.1.call-update) | async-done | bytes 8388624 | tf_op jit(solution)/shard_map/all_gather | solution.py:126
  158.9 6.4 %fusion.34 = bf16[1024,128]{0,1:T(8,128)(2,1)S(1)} fusion(bf16[4096,128]{1,0:T(8,128)(2,1)S(1)} %bitcast.238, bf16[1024,4096]{1,0:T(8,128)(2,1)} %all-gather.5.cloned.1.call-done), kind=kOutput, calls=%fused_computation.58 | convolution fusion | flops 1073872896 | bytes 9699328 | tf_op jit(solution)/shard_map/dot_general | solution.py:143
  165.3 2.1 collective-permute-start.8
  167.5 4.1 %fusion.20 = bf16[1024,256]{0,1:T(8,128)(2,1)S(1)} fusion(bf16[4096,256]{1,0:T(8,128)(2,1)} %bitcast.242, bf16[1024,4096]{1,0:T(8,128)(2,1)S(1)} %copy-done.1), kind=kOutput, calls=%fused_computation.39 | convolution fusion | flops 2147745792 | bytes 11010048 | tf_op jit(solution)/shard_map/dot_general | solution.py:145
  171.6 3.2 %fusion.21 = bf16[1024,256]{0,1:T(8,128)(2,1)} fusion(bf16[4096,256]{1,0:T(8,128)(2,1)S(1)} %bitcast.243, bf16[1024,4096]{1,0:T(8,128)(2,1)S(1)} %copy-done.1), kind=kOutput, calls=%fused_computation.40 | convolution fusion | flops 2147745792 | bytes 11010048 | tf_op jit(solution)/shard_map/dot_general | solution.py:186
  175.1 3.9 %collective-permute-start.9 = (bf16[3,512]{0,1:T(8,128)(2,1)S(1)}, bf16[3,512]{0,1:T(8,128)(2,1)S(1)}, u32[]{:S(2)}, u32[]{:S(2)}) collective-permute-start(bf16[3,512]{0,1:T(8,128)(2,1)S(1)} %pad_maximum_fusion.6), channel_id=1, source_target_pairs={{0,32},{32,64},{64,96},{96,128},{128,160},{160,192},{192,224},{224... | collective-permute-start | bytes 9224 | tf_op jit(solution)/shard_map/ppermute | solution.py:23
  179.0 2.3 broadcast_multiply_fusion
  181.3 1.3 collective-permute-done.9
  183.0 1.2 multiply_convert_fusion.3
  185.7 34.4 %while.16 = (s32[]{:T(128)}, f32[4,256,256]{1,2,0:T(8,128)}, f32[4,128,256]{2,1,0:T(8,128)}, f32[4,4]{1,0:T(4,128)S(1)}, f32[4,4,256]{2,1,0:T(4,128)S(1)}, /*ind...) while((s32[]{:T(128)}, f32[4,256,256]{1,2,0:T(8,128)}, ...), condition=%wide.region_5.6_spmd, body=%wide.region_2.5_spmd.sunk | while | flops 69210640 | bytes 2653675 | solution.py:170
  187.0 1.4 compare_reduce_fusion.3
  188.4 1.2 reduce-window.22
  195.6 1.4 compare_reduce_fusion.3
  197.0 1.2 reduce-window.22
  204.2 1.4 compare_reduce_fusion.3
  205.7 1.2 reduce-window.22
  212.8 1.4 compare_reduce_fusion.3
  214.3 1.2 reduce-window.22
  221.9 3.7 %collective-permute-start.10 = (f32[136,256]{1,0:T(8,128)S(1)}, f32[136,256]{1,0:T(8,128)S(1)}, u32[]{:S(2)}, u32[]{:S(2)}) collective-permute-start(f32[136,256]{1,0:T(8,128)S(1)} %pad_maximum_fusion.4), channel_id=1, source_target_pairs={{0,32},{32,64},{64,96},{96,128},{128,160},{160,192},{192,224},{224... | collective-permute-start | bytes 417800 | tf_op jit(solution)/shard_map/ppermute | solution.py:23
  225.6 6.9 %collective-permute-start.11 = (f32[136,256]{1,0:T(8,128)S(1)}, f32[136,256]{1,0:T(8,128)S(1)}, u32[]{:S(2)}, u32[]{:S(2)}) collective-permute-start(f32[136,256]{1,0:T(8,128)S(1)} %pad_maximum_fusion.4), channel_id=1, source_target_pairs={{0,64},{32,96},{64,128},{96,160},{128,192},{160,224},{192,256},{22... | collective-permute-start | bytes 417800 | tf_op jit(solution)/shard_map/ppermute | solution.py:23
  232.5 2.0 collective-permute-start.12
  234.7 2.9 collective-permute-done.10
  237.5 24.1 %collective-permute-done.11 = f32[136,256]{1,0:T(8,128)S(1)} collective-permute-done((f32[136,256]{1,0:T(8,128)S(1)}, f32[136,256]{1,0:T(8,128)S(1)}, u32[]{:S(2)}, u32[]{:S(2)}) %collective-permute-start.11) | collective-permute-done | bytes 139296 | tf_op jit(solution)/shard_map/ppermute | solution.py:23
  261.7 2.4 collective-permute-done.12
  264.2 5.1 %collective-permute-start.13 = (f32[136,256]{1,0:T(8,128)S(1)}, f32[136,256]{1,0:T(8,128)S(1)}, u32[]{:S(2)}, u32[]{:S(2)}) collective-permute-start(f32[136,256]{1,0:T(8,128)S(1)} %pad_maximum_fusion.5), channel_id=1, source_target_pairs={{0,32},{32,64},{64,96},{96,128},{128,160},{160,192},{192,224},{224... | collective-permute-start | bytes 417800 | tf_op jit(solution)/shard_map/ppermute | solution.py:23
  269.3 1.9 collective-permute-start.14
  272.1 14.6 %collective-permute-done.14 = f32[136,256]{1,0:T(8,128)S(1)} collective-permute-done((f32[136,256]{1,0:T(8,128)S(1)}, f32[136,256]{1,0:T(8,128)S(1)}, u32[]{:S(2)}, u32[]{:S(2)}) %collective-permute-start.14) | collective-permute-done | bytes 139296 | tf_op jit(solution)/shard_map/ppermute | solution.py:23
  286.8 1.3 fusion.38
  (209 shorter events, 36.8 us)
Async XLA Ops:
  6.5 1.2 copy-start
  6.5 31.0 %copy-start.6 = (s32[16]{0:T(128)S(1)}, s32[16]{0:T(128)}, u32[]{:S(2)}) copy-start(s32[16]{0:T(128)} %param.13) | copy-start | bytes 196
  6.5 31.4 %copy-start.4 = (f32[4,256]{1,0:T(4,128)S(1)}, f32[4,256]{1,0:T(4,128)}, u32[]{:S(2)}) copy-start(f32[4,256]{1,0:T(4,128)} %param.18) | copy-start | bytes 12292
  6.5 31.5 %copy-start.8 = (f32[4]{0:T(128)S(1)}, f32[4]{0:T(128)}, u32[]{:S(2)}) copy-start(f32[4]{0:T(128)} %param.21) | copy-start | bytes 52
  6.5 99.7 %all-gather.7.cloned.1.call-start = ((), (), s32[]{:S(2)}) async-start(), calls=%async_computation.1 | async-start | bytes 2359296 | tf_op jit(solution)/shard_map/all_gather | solution.py:135
  30.6 128.3 %all-gather.5.cloned.1.call-start = ((), (), s32[]{:S(2)}) async-start(), calls=%async_computation | async-start | bytes 8650752 | tf_op jit(solution)/shard_map/all_gather | solution.py:126
  31.4 12.1 %collective-permute-start = (bf16[2,392,256]{2,1,0:T(8,128)(2,1)S(1)}, bf16[2,392,256]{2,1,0:T(8,128)(2,1)S(1)}, u32[]{:S(2)}, u32[]{:S(2)}) collective-permute-start(bf16[2,392,256]{2,1,0:T(8,128)(2,1)S(1)} %slice.371), channel_id=1, source_target_pairs={{0,32},{32,64},{64,96},{96,128},{128,160},{160,192},{192,224},{224... | collective-permute-start | bytes 1204232 | tf_op jit(solution)/shard_map/ppermute | solution.py:37
  35.6 12.4 %collective-permute-start.1 = (bf16[2,392,256]{2,1,0:T(8,128)(2,1)S(1)}, bf16[2,392,256]{2,1,0:T(8,128)(2,1)S(1)}, u32[]{:S(2)}, u32[]{:S(2)}) collective-permute-start(bf16[2,392,256]{2,1,0:T(8,128)(2,1)S(1)} %slice.371), channel_id=1, source_target_pairs={{0,224},{32,0},{64,32},{96,64},{128,96},{160,128},{192,160},{224,1... | collective-permute-start | bytes 1204232 | tf_op jit(solution)/shard_map/ppermute | solution.py:38
  43.4 23.8 %collective-permute-start.2 = (bf16[2,392,256]{2,1,0:T(8,128)(2,1)S(1)}, bf16[2,392,256]{2,1,0:T(8,128)(2,1)S(1)}, u32[]{:S(2)}, u32[]{:S(2)}) collective-permute-start(bf16[2,392,256]{2,1,0:T(8,128)(2,1)S(1)} %collective-permute-done), channel_id=1, source_target_pairs={{0,32},{32,64},{64,96},{96,128},{128,160},{160,192},{192,224},{224... | collective-permute-start | bytes 1204232 | tf_op jit(solution)/shard_map/ppermute | solution.py:37
  48.1 23.2 %collective-permute-start.3 = (bf16[2,392,256]{2,1,0:T(8,128)(2,1)S(1)}, bf16[2,392,256]{2,1,0:T(8,128)(2,1)S(1)}, u32[]{:S(2)}, u32[]{:S(2)}) collective-permute-start(bf16[2,392,256]{2,1,0:T(8,128)(2,1)S(1)} %collective-permute-done.1), channel_id=1, source_target_pairs={{0,224},{32,0},{64,32},{96,64},{128,96},{160,128},{192,160},{224,1... | collective-permute-start | bytes 1204232 | tf_op jit(solution)/shard_map/ppermute | solution.py:38
  67.2 21.6 %collective-permute-start.4 = (bf16[2,392,256]{2,1,0:T(8,128)(2,1)S(1)}, bf16[2,392,256]{2,1,0:T(8,128)(2,1)S(1)}, u32[]{:S(2)}, u32[]{:S(2)}) collective-permute-start(bf16[2,392,256]{2,1,0:T(8,128)(2,1)S(1)} %collective-permute-done.2), channel_id=1, source_target_pairs={{0,32},{32,64},{64,96},{96,128},{128,160},{160,192},{192,224},{224... | collective-permute-start | bytes 1204232 | tf_op jit(solution)/shard_map/ppermute | solution.py:37
  71.3 19.5 %collective-permute-start.5 = (bf16[2,392,256]{2,1,0:T(8,128)(2,1)S(1)}, bf16[2,392,256]{2,1,0:T(8,128)(2,1)S(1)}, u32[]{:S(2)}, u32[]{:S(2)}) collective-permute-start(bf16[2,392,256]{2,1,0:T(8,128)(2,1)S(1)} %collective-permute-done.3), channel_id=1, source_target_pairs={{0,224},{32,0},{64,32},{96,64},{128,96},{160,128},{192,160},{224,1... | collective-permute-start | bytes 1204232 | tf_op jit(solution)/shard_map/ppermute | solution.py:38
  88.8 8.0 %collective-permute-start.6 = (bf16[2,196,256]{2,1,0:T(8,128)(2,1)S(1)}, bf16[2,196,256]{2,1,0:T(8,128)(2,1)S(1)}, u32[]{:S(2)}, u32[]{:S(2)}) collective-permute-start(bf16[2,196,256]{2,1,0:T(8,128)(2,1)S(1)} %slice.372), channel_id=1, source_target_pairs={{0,32},{32,64},{64,96},{96,128},{128,160},{160,192},{192,224},{224... | collective-permute-start | bytes 602120 | tf_op jit(solution)/shard_map/ppermute | solution.py:41
  90.8 8.1 %collective-permute-start.7 = (bf16[2,196,256]{2,1,0:T(8,128)(2,1)S(1)}, bf16[2,196,256]{2,1,0:T(8,128)(2,1)S(1)}, u32[]{:S(2)}, u32[]{:S(2)}) collective-permute-start(bf16[2,196,256]{2,1,0:T(8,128)(2,1)S(1)} %slice.373), channel_id=1, source_target_pairs={{0,224},{32,0},{64,32},{96,64},{128,96},{160,128},{192,160},{224,1... | collective-permute-start | bytes 602120 | tf_op jit(solution)/shard_map/ppermute | solution.py:42
  158.9 8.6 %copy-start.1 = (bf16[1024,4096]{1,0:T(8,128)(2,1)S(1)}, bf16[1024,4096]{1,0:T(8,128)(2,1)}, u32[]{:S(2)}) copy-start(bf16[1024,4096]{1,0:T(8,128)(2,1)} %all-gather.5.cloned.1.call-done) | copy-start | bytes 25165828
  165.3 9.6 %collective-permute-start.8 = (bf16[1024,128]{0,1:T(8,128)(2,1)S(1)}, bf16[1024,128]{0,1:T(8,128)(2,1)S(1)}, u32[]{:S(2)}, u32[]{:S(2)}) collective-permute-start(bf16[1024,128]{0,1:T(8,128)(2,1)S(1)} %fusion.34), channel_id=1, source_target_pairs={{0,1},{1,0},{2,3},{3,2},{4,5},{5,4},{6,7},{7,6},{8,9},{9,8},{10,11... | collective-permute-start | bytes 786440 | tf_op jit(solution)/shard_map/ppermute | solution.py:144
  167.5 4.1 %copy-start.2 = (bf16[2,8,256,256]{3,2,1,0:T(8,128)(2,1)S(1)}, bf16[2,8,256,256]{3,2,1,0:T(8,128)(2,1)}, u32[]{:S(2)}) copy-start(bf16[2,8,256,256]{3,2,1,0:T(8,128)(2,1)} %copy.121) | copy-start | bytes 6291460
  171.6 7.4 %copy-start.5 = (f32[4]{0:T(128)S(1)}, f32[4]{0:T(128)}, u32[]{:S(2)}) copy-start(f32[4]{0:T(128)} %param.20) | copy-start | bytes 52
  175.1 7.6 %collective-permute-start.9 = (bf16[3,512]{0,1:T(8,128)(2,1)S(1)}, bf16[3,512]{0,1:T(8,128)(2,1)S(1)}, u32[]{:S(2)}, u32[]{:S(2)}) collective-permute-start(bf16[3,512]{0,1:T(8,128)(2,1)S(1)} %pad_maximum_fusion.6), channel_id=1, source_target_pairs={{0,32},{32,64},{64,96},{96,128},{128,160},{160,192},{192,224},{224... | collective-permute-start | bytes 9224 | tf_op jit(solution)/shard_map/ppermute | solution.py:23
  220.1 68.1 %copy-start.3 = (f32[4,128,256]{2,1,0:T(8,128)S(1)}, f32[4,128,256]{2,1,0:T(8,128)}, u32[]{:S(2)}) copy-start(f32[4,128,256]{2,1,0:T(8,128)} %get-tuple-element.72) | copy-start | bytes 1572868
  221.9 15.7 %collective-permute-start.10 = (f32[136,256]{1,0:T(8,128)S(1)}, f32[136,256]{1,0:T(8,128)S(1)}, u32[]{:S(2)}, u32[]{:S(2)}) collective-permute-start(f32[136,256]{1,0:T(8,128)S(1)} %pad_maximum_fusion.4), channel_id=1, source_target_pairs={{0,32},{32,64},{64,96},{96,128},{128,160},{160,192},{192,224},{224... | collective-permute-start | bytes 417800 | tf_op jit(solution)/shard_map/ppermute | solution.py:23
  225.6 36.1 %collective-permute-start.11 = (f32[136,256]{1,0:T(8,128)S(1)}, f32[136,256]{1,0:T(8,128)S(1)}, u32[]{:S(2)}, u32[]{:S(2)}) collective-permute-start(f32[136,256]{1,0:T(8,128)S(1)} %pad_maximum_fusion.4), channel_id=1, source_target_pairs={{0,64},{32,96},{64,128},{96,160},{128,192},{160,224},{192,256},{22... | collective-permute-start | bytes 417800 | tf_op jit(solution)/shard_map/ppermute | solution.py:23
  232.5 31.6 %collective-permute-start.12 = (f32[136,256]{1,0:T(8,128)S(1)}, f32[136,256]{1,0:T(8,128)S(1)}, u32[]{:S(2)}, u32[]{:S(2)}) collective-permute-start(f32[136,256]{1,0:T(8,128)S(1)} %pad_maximum_fusion.4), channel_id=1, source_target_pairs={{0,96},{32,128},{64,160},{96,192},{128,224},{160,256},{192,288},{2... | collective-permute-start | bytes 417800 | tf_op jit(solution)/shard_map/ppermute | solution.py:23
  234.7 53.5 %copy-start.7 = (f32[4,256,256]{1,2,0:T(8,128)S(1)}, f32[4,256,256]{1,2,0:T(8,128)}, u32[]{:S(2)}) copy-start(f32[4,256,256]{1,2,0:T(8,128)} %get-tuple-element.70) | copy-start | bytes 3145732
  234.7 53.5 %copy-start.9 = (bf16[1024,256]{0,1:T(8,128)(2,1)S(1)}, bf16[1024,256]{0,1:T(8,128)(2,1)}, u32[]{:S(2)}) copy-start(bf16[1024,256]{0,1:T(8,128)(2,1)} %fusion.21) | copy-start | bytes 1572868
  264.2 7.9 %collective-permute-start.13 = (f32[136,256]{1,0:T(8,128)S(1)}, f32[136,256]{1,0:T(8,128)S(1)}, u32[]{:S(2)}, u32[]{:S(2)}) collective-permute-start(f32[136,256]{1,0:T(8,128)S(1)} %pad_maximum_fusion.5), channel_id=1, source_target_pairs={{0,32},{32,64},{64,96},{96,128},{128,160},{160,192},{192,224},{224... | collective-permute-start | bytes 417800 | tf_op jit(solution)/shard_map/ppermute | solution.py:23
  269.3 17.4 %collective-permute-start.14 = (f32[136,256]{1,0:T(8,128)S(1)}, f32[136,256]{1,0:T(8,128)S(1)}, u32[]{:S(2)}, u32[]{:S(2)}) collective-permute-start(f32[136,256]{1,0:T(8,128)S(1)} %pad_maximum_fusion.5), channel_id=1, source_target_pairs={{0,160},{32,192},{64,224},{96,256},{128,288},{160,320},{192,352},{... | collective-permute-start | bytes 417800 | tf_op jit(solution)/shard_map/ppermute | solution.py:23
Sparse Core Ops, SparseCore 0:
  30.7 56.6 all-gather.6
  89.6 69.2 all-gather.4
where the time goes:
time: 298 us; the launch traced here: 297 us
  waiting for transfers between devices  120 us (40%)
  starting transfers between devices  58.9 us (20%)
  local copies, waits for them, and re-layouts  35.8 us (12%)
  matrix products  24.7 us (8%)
  blocking collectives  21 us (7%)
  other arithmetic  17.4 us (6%)
  between operations  14.1 us (5%)
  loops' own time  5.8 us (2%)
    all_gather x1, waiting for transfers between devices, local(): gathered = lax.all_gather(tokens, HEAD, axis=0, tiled=True)  49.4 us
    ppermute x6, waiting for transfers between devices, along_seq(): lax.ppermute(value, SEQ, [(i, i + step) for i in range(YH * Z - step)])  46.3 us
    ppermute x6, starting transfers between devices, along_seq(): lax.ppermute(value, SEQ, [(i, i + step) for i in range(YH * Z - step)])  23.6 us
    all_gather x1, blocking collectives, local(): both = lax.all_gather(pack, 'yh', axis=0, tiled=False)  21 us
    ppermute x3, waiting for transfers between devices, ring_gather(): right = lax.ppermute(right, 'z', ring(Z, 1))  20.9 us
    ppermute x3, starting transfers between devices, ring_gather(): left = lax.ppermute(left, 'z', ring(Z, -1))  15.9 us
    ppermute x3, starting transfers between devices, ring_gather(): right = lax.ppermute(right, 'z', ring(Z, 1))  11.3 us
    dynamic_update_slice x9, local copies, waits for them, and re-layouts, put(): lax.dynamic_update_slice(held, piece[None], ((z + offset) % Z, 0, row, 0))  9.48 us
  transfers between devices with their start and end apart: 17, of which 13 were waited for; matrix products, arithmetic and copies ran while one was open for 11% of the time, Pallas kernels for 0%

commit v1 on v0

--- a/solution.py
+++ b/solution.py
@@ -123,7 +123,9 @@
     cols = value_weight.shape[1]
     core = lax.axis_index("c")
     group = lax.axis_index("x") * 2 + lax.axis_index("y") // 2
-    gathered = lax.all_gather(tokens, HEAD, axis=0, tiled=True)
+    gathered = jnp.concatenate(
+        lax.all_to_all(jnp.stack([tokens] * lax.axis_size(HEAD)), HEAD, 0, 0), axis=0
+    )
     state_own = lax.dynamic_index_in_dim(state_weight, group, 0, keepdims=False)
     conv_own = lax.dynamic_index_in_dim(state_conv, group, 0, keepdims=False)
     state_half = jnp.where(core == 0, state_own[:, :STATE], state_own[:, STATE:])

time: 298 us -> 385 us (1.29)
  the two profiles are of different devices: /device:TPU:112 before, /device:TPU:32 now
where the time goes in v1:
time: 385 us; the launch traced here: 384 us
  blocking collectives  157 us (41%)
  waiting for transfers between devices  67.6 us (18%)
  starting transfers between devices  52.7 us (14%)
  local copies, waits for them, and re-layouts  39.3 us (10%)
  matrix products  33.3 us (9%)
  other arithmetic  15.3 us (4%)
  between operations  14.2 us (4%)
  loops' own time  4.76 us (1%)
    all_gather x1, blocking collectives, local(): both = lax.all_gather(pack, 'yh', axis=0, tiled=False)  157 us
    ppermute x6, waiting for transfers between devices, along_seq(): lax.ppermute(value, SEQ, [(i, i + step) for i in range(YH * Z - step)])  42.1 us
    ppermute x3, waiting for transfers between devices, ring_gather(): right = lax.ppermute(right, 'z', ring(Z, 1))  21.8 us
    ppermute x3, starting transfers between devices, ring_gather(): left = lax.ppermute(left, 'z', ring(Z, -1))  19.7 us
    ppermute x6, starting transfers between devices, along_seq(): lax.ppermute(value, SEQ, [(i, i + step) for i in range(YH * Z - step)])  12.9 us
    dynamic_update_slice x9, local copies, waits for them, and re-layouts, put(): lax.dynamic_update_slice(held, piece[None], ((z + offset) % Z, 0, row, 0))  9.51 us
  transfers between devices with their start and end apart: 17, of which 12 were waited for; matrix products, arithmetic and copies ran while one was open for 11% of the time, Pallas kernels for 0%

profile of v1, /device:TPU:32, one launch (start us, length us, event | category | flops | bytes accessed | tf_op | source)
XLA Modules:
  0.0 384.0 jit_solution(3688036563972074042)
XLA Ops:
  6.5 5.3 %stack.8 = bf16[32,32,4096]{2,1,0:T(8,128)(2,1)} broadcast(bf16[32,4096]{1,0:T(8,128)(2,1)} %param.12), dimensions={1,2} | broadcast | bytes 8650752 | tf_op jit(solution)/shard_map/stack | solution.py:127
  11.8 5.3 %all-to-all-start = ((bf16[32,32,4096]{2,1,0:T(8,128)(2,1)}), bf16[32,32,4096]{2,1,0:T(8,128)(2,1)}, u32[]{:S(2)}, u32[]{:S(2)}) async-start(bf16[32,32,4096]{2,1,0:T(8,128)(2,1)} %stack.8), calls=%async_computation | async-start | bytes 16777216 | tf_op jit(solution)/shard_map/all_to_all | solution.py:127
  17.4 156.9 %all-gather = bf16[1296,256]{1,0:T(8,128)(2,1)S(1)} all-gather(bf16[648,256]{1,0:T(8,128)(2,1)S(1)} %fusion.47), channel_id=2, replica_groups=mesh['yh'=2,'z'=8,'x'=4,'y'=4,'c'=2] {'yh'}, dimensions={0}, use_global_device_ids=true | all-gather | bytes 995328 | tf_op jit(solution)/shard_map/all_gather | solution.py:135
  175.0 1.9 collective-permute-start
  177.0 8.6 %collective-permute-start.1 = (bf16[2,392,256]{2,1,0:T(8,128)(2,1)S(1)}, bf16[2,392,256]{2,1,0:T(8,128)(2,1)S(1)}, u32[]{:S(2)}, u32[]{:S(2)}) collective-permute-start(bf16[2,392,256]{2,1,0:T(8,128)(2,1)S(1)} %slice.371), channel_id=1, source_target_pairs={{0,224},{32,0},{64,32},{96,64},{128,96},{160,128},{192,160},{224,1... | collective-permute-start | bytes 1204232 | tf_op jit(solution)/shard_map/ppermute | solution.py:38
  187.2 1.9 broadcast_in_dim.172
  189.9 3.0 collective-permute-done
  192.9 1.9 collective-permute-start.2
  194.8 2.4 collective-permute-done.1
  197.2 5.6 %collective-permute-start.3 = (bf16[2,392,256]{2,1,0:T(8,128)(2,1)S(1)}, bf16[2,392,256]{2,1,0:T(8,128)(2,1)S(1)}, u32[]{:S(2)}, u32[]{:S(2)}) collective-permute-start(bf16[2,392,256]{2,1,0:T(8,128)(2,1)S(1)} %collective-permute-done.1), channel_id=1, source_target_pairs={{0,224},{32,0},{64,32},{96,64},{128,96},{160,128},{192,160},{224,1... | collective-permute-start | bytes 1204232 | tf_op jit(solution)/shard_map/ppermute | solution.py:38
  204.4 11.3 %collective-permute-done.2 = bf16[2,392,256]{2,1,0:T(8,128)(2,1)S(1)} collective-permute-done((bf16[2,392,256]{2,1,0:T(8,128)(2,1)S(1)}, bf16[2,392,256]{2,1,0:T(8,128)(2,1)S(1)}, u32[]{:S(2)}, u32[]{:S(2)}) %collective-permute-start.2) | collective-permute-done | bytes 401440 | tf_op jit(solution)/shard_map/ppermute | solution.py:37
  215.7 1.9 collective-permute-start.4
  218.4 5.6 %collective-permute-start.5 = (bf16[2,392,256]{2,1,0:T(8,128)(2,1)S(1)}, bf16[2,392,256]{2,1,0:T(8,128)(2,1)S(1)}, u32[]{:S(2)}, u32[]{:S(2)}) collective-permute-start(bf16[2,392,256]{2,1,0:T(8,128)(2,1)S(1)} %collective-permute-done.3), channel_id=1, source_target_pairs={{0,224},{32,0},{64,32},{96,64},{128,96},{160,128},{192,160},{224,1... | collective-permute-start | bytes 1204232 | tf_op jit(solution)/shard_map/ppermute | solution.py:38
  225.6 7.5 %collective-permute-done.4 = bf16[2,392,256]{2,1,0:T(8,128)(2,1)S(1)} collective-permute-done((bf16[2,392,256]{2,1,0:T(8,128)(2,1)S(1)}, bf16[2,392,256]{2,1,0:T(8,128)(2,1)S(1)}, u32[]{:S(2)}, u32[]{:S(2)}) %collective-permute-start.4) | collective-permute-done | bytes 401440 | tf_op jit(solution)/shard_map/ppermute | solution.py:37
  233.1 2.1 collective-permute-start.6
  235.2 5.0 %collective-permute-start.7 = (bf16[2,196,256]{2,1,0:T(8,128)(2,1)S(1)}, bf16[2,196,256]{2,1,0:T(8,128)(2,1)S(1)}, u32[]{:S(2)}, u32[]{:S(2)}) collective-permute-start(bf16[2,196,256]{2,1,0:T(8,128)(2,1)S(1)} %slice.373), channel_id=1, source_target_pairs={{0,224},{32,0},{64,32},{96,64},{128,96},{160,128},{192,160},{224,1... | collective-permute-start | bytes 602120 | tf_op jit(solution)/shard_map/ppermute | solution.py:42
  242.3 2.1 dynamic_update_slice.50
  244.4 1.8 dynamic_update_slice.51
  246.3 3.1 slice.374
  250.2 1.3 slice_bitcast_fusion.1
  251.7 3.1 copy.121
  254.9 6.4 %fusion.34 = bf16[1024,128]{0,1:T(8,128)(2,1)S(1)} fusion(bf16[4096,128]{1,0:T(8,128)(2,1)S(1)} %bitcast.239, bf16[1024,4096]{1,0:T(8,128)(2,1)} %bitcast.38), kind=kOutput, calls=%fused_computation.58 | convolution fusion | flops 1073872896 | bytes 9699328 | tf_op jit(solution)/shard_map/dot_general | solution.py:145
  261.3 1.9 collective-permute-start.8
  263.2 5.9 %fusion.20 = bf16[1024,256]{0,1:T(8,128)(2,1)S(1)} fusion(bf16[4096,256]{1,0:T(8,128)(2,1)S(1)} %bitcast.243, bf16[1024,4096]{1,0:T(8,128)(2,1)} %bitcast.38), kind=kOutput, calls=%fused_computation.39 | convolution fusion | flops 2147745792 | bytes 11010048 | tf_op jit(solution)/shard_map/dot_general | solution.py:147
  269.2 6.7 %fusion.21 = bf16[1024,256]{0,1:T(8,128)(2,1)} fusion(bf16[4096,256]{1,0:T(8,128)(2,1)S(1)} %bitcast.244, bf16[1024,4096]{1,0:T(8,128)(2,1)} %bitcast.38), kind=kOutput, calls=%fused_computation.40 | convolution fusion | flops 2147745792 | bytes 11010048 | tf_op jit(solution)/shard_map/dot_general | solution.py:188
  276.1 2.1 collective-permute-start.9
  278.2 5.7 %broadcast_multiply_fusion = (f32[1024,4]{0,1:T(4,128)S(1)}, f32[1024,4]{0,1:T(4,128)S(1)}) fusion(f32[4]{0:T(128)S(1)} %exponential_negate_fusion, f32[4]{0:T(128)S(1)} %copy-done.8, bf16[1024,4096]{1,0:T(8,128)(2,1)} %bitcast.38, bf16[4096,8]{0,1:T(8,128)(2,1)S(1)} %bitcast.247), kind=kOutput, calls=%fused_computation.155 | convolution fusion | flops 33595392 | bytes 8455168 | tf_op jit(solution)/shard_map/dot_general | solution.py:148
  283.9 6.0 %collective-permute-done.9 = bf16[3,512]{0,1:T(8,128)(2,1)S(1)} collective-permute-done((bf16[3,512]{0,1:T(8,128)(2,1)S(1)}, bf16[3,512]{0,1:T(8,128)(2,1)S(1)}, u32[]{:S(2)}, u32[]{:S(2)}) %collective-permute-start.9) | collective-permute-done | bytes 3104 | tf_op jit(solution)/shard_map/ppermute | solution.py:23
  292.9 31.6 %while.16 = (s32[]{:T(128)}, f32[4,256,256]{1,2,0:T(8,128)}, f32[4,128,256]{2,1,0:T(8,128)}, f32[4,4]{1,0:T(4,128)S(1)}, f32[4,4,256]{2,1,0:T(4,128)S(1)}, /*ind...) while((s32[]{:T(128)}, f32[4,256,256]{1,2,0:T(8,128)}, ...), condition=%wide.region_5.6_spmd, body=%wide.region_2.5_spmd.sunk | while | flops 69210640 | bytes 2653675 | solution.py:172
  294.1 1.1 compare_reduce_fusion.3
  295.2 1.2 reduce-window.22
  302.0 1.1 compare_reduce_fusion.3
  303.1 1.2 reduce-window.22
  309.9 1.1 compare_reduce_fusion.3
  311.0 1.2 reduce-window.22
  317.8 1.1 compare_reduce_fusion.3
  319.0 1.2 reduce-window.22
  326.3 1.9 collective-permute-start.10
  328.3 1.9 collective-permute-start.11
  330.2 3.1 collective-permute-start.12
  333.5 8.4 %collective-permute-done.10 = f32[136,256]{1,0:T(8,128)S(1)} collective-permute-done((f32[136,256]{1,0:T(8,128)S(1)}, f32[136,256]{1,0:T(8,128)S(1)}, u32[]{:S(2)}, u32[]{:S(2)}) %collective-permute-start.10) | collective-permute-done | bytes 139296 | tf_op jit(solution)/shard_map/ppermute | solution.py:23
  341.9 8.1 %collective-permute-done.11 = f32[136,256]{1,0:T(8,128)S(1)} collective-permute-done((f32[136,256]{1,0:T(8,128)S(1)}, f32[136,256]{1,0:T(8,128)S(1)}, u32[]{:S(2)}, u32[]{:S(2)}) %collective-permute-start.11) | collective-permute-done | bytes 139296 | tf_op jit(solution)/shard_map/ppermute | solution.py:23
  350.0 5.0 %collective-permute-done.12 = f32[136,256]{1,0:T(8,128)S(1)} collective-permute-done((f32[136,256]{1,0:T(8,128)S(1)}, f32[136,256]{1,0:T(8,128)S(1)}, u32[]{:S(2)}, u32[]{:S(2)}) %collective-permute-start.12) | collective-permute-done | bytes 139296 | tf_op jit(solution)/shard_map/ppermute | solution.py:23
  355.1 1.9 collective-permute-start.13
  357.0 1.9 collective-permute-start.14
  359.0 9.3 %collective-permute-done.13 = f32[136,256]{1,0:T(8,128)S(1)} collective-permute-done((f32[136,256]{1,0:T(8,128)S(1)}, f32[136,256]{1,0:T(8,128)S(1)}, u32[]{:S(2)}, u32[]{:S(2)}) %collective-permute-start.13) | collective-permute-done | bytes 139296 | tf_op jit(solution)/shard_map/ppermute | solution.py:23
  368.3 5.2 %collective-permute-done.14 = f32[136,256]{1,0:T(8,128)S(1)} collective-permute-done((f32[136,256]{1,0:T(8,128)S(1)}, f32[136,256]{1,0:T(8,128)S(1)}, u32[]{:S(2)}, u32[]{:S(2)}) %collective-permute-start.14) | collective-permute-done | bytes 139296 | tf_op jit(solution)/shard_map/ppermute | solution.py:23
  373.6 1.3 fusion.38
  (215 shorter events, 35.2 us)
Async XLA Ops:
  6.5 10.7 %copy-start = (bf16[8,256,256]{2,1,0:T(8,128)(2,1)S(1)}, bf16[8,256,256]{2,1,0:T(8,128)(2,1)}, u32[]{:S(2)}) copy-start(bf16[8,256,256]{2,1,0:T(8,128)(2,1)} %param.16) | copy-start | bytes 3145732
  11.8 5.5 %copy-start.4 = (bf16[256,256]{1,0:T(8,128)(2,1)S(1)}, bf16[256,256]{1,0:T(8,128)(2,1)}, u32[]{:S(2)}) copy-start(bf16[256,256]{1,0:T(8,128)(2,1)} %param.15) | copy-start | bytes 393220
  11.8 5.5 %copy-start.5 = (bf16[256,256]{1,0:T(8,128)(2,1)S(1)}, bf16[256,256]{1,0:T(8,128)(2,1)}, u32[]{:S(2)}) copy-start(bf16[256,256]{1,0:T(8,128)(2,1)} %param.14) | copy-start | bytes 393220
  11.8 5.5 %copy-start.7 = (bf16[256,4]{0,1:T(4,128)(2,1)S(1)}, bf16[256,4]{0,1:T(4,128)(2,1)}, u32[]{:S(2)}) copy-start(bf16[256,4]{0,1:T(4,128)(2,1)} %param.17) | copy-start | bytes 6148
  11.8 243.0 %all-to-all-start = ((bf16[32,32,4096]{2,1,0:T(8,128)(2,1)}), bf16[32,32,4096]{2,1,0:T(8,128)(2,1)}, u32[]{:S(2)}, u32[]{:S(2)}) async-start(bf16[32,32,4096]{2,1,0:T(8,128)(2,1)} %stack.8), calls=%async_computation | async-start | bytes 16777216 | tf_op jit(solution)/shard_map/all_to_all | solution.py:127
  17.1 168.4 %copy-start.9 = (s32[16]{0:T(128)S(1)}, s32[16]{0:T(128)}, u32[]{:S(2)}) copy-start(s32[16]{0:T(128)} %param.13) | copy-start | bytes 196
  17.2 168.8 %copy-start.6 = (f32[4,256]{1,0:T(4,128)S(1)}, f32[4,256]{1,0:T(4,128)}, u32[]{:S(2)}) copy-start(f32[4,256]{1,0:T(4,128)} %param.18) | copy-start | bytes 12292
  17.2 168.9 %copy-start.11 = (f32[4]{0:T(128)S(1)}, f32[4]{0:T(128)}, u32[]{:S(2)}) copy-start(f32[4]{0:T(128)} %param.21) | copy-start | bytes 52
  17.2 234.5 %all-gather.4.cloned.1.call-start = ((), (), s32[]{:S(2)}) async-start(), calls=%async_computation.1 | async-start | bytes 2359296 | tf_op jit(solution)/shard_map/all_gather | solution.py:137
  175.0 17.8 %collective-permute-start = (bf16[2,392,256]{2,1,0:T(8,128)(2,1)S(1)}, bf16[2,392,256]{2,1,0:T(8,128)(2,1)S(1)}, u32[]{:S(2)}, u32[]{:S(2)}) collective-permute-start(bf16[2,392,256]{2,1,0:T(8,128)(2,1)S(1)} %slice.371), channel_id=1, source_target_pairs={{0,32},{32,64},{64,96},{96,128},{128,160},{160,192},{192,224},{224... | collective-permute-start | bytes 1204232 | tf_op jit(solution)/shard_map/ppermute | solution.py:37
  177.0 20.2 %collective-permute-start.1 = (bf16[2,392,256]{2,1,0:T(8,128)(2,1)S(1)}, bf16[2,392,256]{2,1,0:T(8,128)(2,1)S(1)}, u32[]{:S(2)}, u32[]{:S(2)}) collective-permute-start(bf16[2,392,256]{2,1,0:T(8,128)(2,1)S(1)} %slice.371), channel_id=1, source_target_pairs={{0,224},{32,0},{64,32},{96,64},{128,96},{160,128},{192,160},{224,1... | collective-permute-start | bytes 1204232 | tf_op jit(solution)/shard_map/ppermute | solution.py:38
  192.9 22.8 %collective-permute-start.2 = (bf16[2,392,256]{2,1,0:T(8,128)(2,1)S(1)}, bf16[2,392,256]{2,1,0:T(8,128)(2,1)S(1)}, u32[]{:S(2)}, u32[]{:S(2)}) collective-permute-start(bf16[2,392,256]{2,1,0:T(8,128)(2,1)S(1)} %collective-permute-done), channel_id=1, source_target_pairs={{0,32},{32,64},{64,96},{96,128},{128,160},{160,192},{192,224},{224... | collective-permute-start | bytes 1204232 | tf_op jit(solution)/shard_map/ppermute | solution.py:37
  197.2 21.2 %collective-permute-start.3 = (bf16[2,392,256]{2,1,0:T(8,128)(2,1)S(1)}, bf16[2,392,256]{2,1,0:T(8,128)(2,1)S(1)}, u32[]{:S(2)}, u32[]{:S(2)}) collective-permute-start(bf16[2,392,256]{2,1,0:T(8,128)(2,1)S(1)} %collective-permute-done.1), channel_id=1, source_target_pairs={{0,224},{32,0},{64,32},{96,64},{128,96},{160,128},{192,160},{224,1... | collective-permute-start | bytes 1204232 | tf_op jit(solution)/shard_map/ppermute | solution.py:38
  215.7 17.4 %collective-permute-start.4 = (bf16[2,392,256]{2,1,0:T(8,128)(2,1)S(1)}, bf16[2,392,256]{2,1,0:T(8,128)(2,1)S(1)}, u32[]{:S(2)}, u32[]{:S(2)}) collective-permute-start(bf16[2,392,256]{2,1,0:T(8,128)(2,1)S(1)} %collective-permute-done.2), channel_id=1, source_target_pairs={{0,32},{32,64},{64,96},{96,128},{128,160},{160,192},{192,224},{224... | collective-permute-start | bytes 1204232 | tf_op jit(solution)/shard_map/ppermute | solution.py:37
  218.4 16.8 %collective-permute-start.5 = (bf16[2,392,256]{2,1,0:T(8,128)(2,1)S(1)}, bf16[2,392,256]{2,1,0:T(8,128)(2,1)S(1)}, u32[]{:S(2)}, u32[]{:S(2)}) collective-permute-start(bf16[2,392,256]{2,1,0:T(8,128)(2,1)S(1)} %collective-permute-done.3), channel_id=1, source_target_pairs={{0,224},{32,0},{64,32},{96,64},{128,96},{160,128},{192,160},{224,1... | collective-permute-start | bytes 1204232 | tf_op jit(solution)/shard_map/ppermute | solution.py:38
  233.1 9.2 %collective-permute-start.6 = (bf16[2,196,256]{2,1,0:T(8,128)(2,1)S(1)}, bf16[2,196,256]{2,1,0:T(8,128)(2,1)S(1)}, u32[]{:S(2)}, u32[]{:S(2)}) collective-permute-start(bf16[2,196,256]{2,1,0:T(8,128)(2,1)S(1)} %slice.372), channel_id=1, source_target_pairs={{0,32},{32,64},{64,96},{96,128},{128,160},{160,192},{192,224},{224... | collective-permute-start | bytes 602120 | tf_op jit(solution)/shard_map/ppermute | solution.py:41
  235.2 9.2 %collective-permute-start.7 = (bf16[2,196,256]{2,1,0:T(8,128)(2,1)S(1)}, bf16[2,196,256]{2,1,0:T(8,128)(2,1)S(1)}, u32[]{:S(2)}, u32[]{:S(2)}) collective-permute-start(bf16[2,196,256]{2,1,0:T(8,128)(2,1)S(1)} %slice.373), channel_id=1, source_target_pairs={{0,224},{32,0},{64,32},{96,64},{128,96},{160,128},{192,160},{224,1... | collective-permute-start | bytes 602120 | tf_op jit(solution)/shard_map/ppermute | solution.py:42
  254.9 8.4 %copy-start.1 = (bf16[2,8,256,256]{3,2,1,0:T(8,128)(2,1)S(1)}, bf16[2,8,256,256]{3,2,1,0:T(8,128)(2,1)}, u32[]{:S(2)}) copy-start(bf16[2,8,256,256]{3,2,1,0:T(8,128)(2,1)} %slice.374) | copy-start | bytes 6291460
  261.3 14.6 %collective-permute-start.8 = (bf16[1024,128]{0,1:T(8,128)(2,1)S(1)}, bf16[1024,128]{0,1:T(8,128)(2,1)S(1)}, u32[]{:S(2)}, u32[]{:S(2)}) collective-permute-start(bf16[1024,128]{0,1:T(8,128)(2,1)S(1)} %fusion.34), channel_id=1, source_target_pairs={{0,1},{1,0},{2,3},{3,2},{4,5},{5,4},{6,7},{7,6},{8,9},{9,8},{10,11... | collective-permute-start | bytes 786440 | tf_op jit(solution)/shard_map/ppermute | solution.py:146
  263.2 5.9 %copy-start.2 = (bf16[2,8,256,256]{3,2,1,0:T(8,128)(2,1)S(1)}, bf16[2,8,256,256]{3,2,1,0:T(8,128)(2,1)}, u32[]{:S(2)}) copy-start(bf16[2,8,256,256]{3,2,1,0:T(8,128)(2,1)} %copy.121) | copy-start | bytes 6291460
  269.2 9.1 %copy-start.8 = (f32[4]{0:T(128)S(1)}, f32[4]{0:T(128)}, u32[]{:S(2)}) copy-start(f32[4]{0:T(128)} %param.20) | copy-start | bytes 52
  276.1 13.8 %collective-permute-start.9 = (bf16[3,512]{0,1:T(8,128)(2,1)S(1)}, bf16[3,512]{0,1:T(8,128)(2,1)S(1)}, u32[]{:S(2)}, u32[]{:S(2)}) collective-permute-start(bf16[3,512]{0,1:T(8,128)(2,1)S(1)} %pad_maximum_fusion.6), channel_id=1, source_target_pairs={{0,32},{32,64},{64,96},{96,128},{128,160},{160,192},{192,224},{224... | collective-permute-start | bytes 9224 | tf_op jit(solution)/shard_map/ppermute | solution.py:23
  324.5 50.4 %copy-start.3 = (f32[4,128,256]{2,1,0:T(8,128)S(1)}, f32[4,128,256]{2,1,0:T(8,128)}, u32[]{:S(2)}) copy-start(f32[4,128,256]{2,1,0:T(8,128)} %get-tuple-element.72) | copy-start | bytes 1572868
  326.3 15.6 %collective-permute-start.10 = (f32[136,256]{1,0:T(8,128)S(1)}, f32[136,256]{1,0:T(8,128)S(1)}, u32[]{:S(2)}, u32[]{:S(2)}) collective-permute-start(f32[136,256]{1,0:T(8,128)S(1)} %pad_maximum_fusion.4), channel_id=1, source_target_pairs={{0,32},{32,64},{64,96},{96,128},{128,160},{160,192},{192,224},{224... | collective-permute-start | bytes 417800 | tf_op jit(solution)/shard_map/ppermute | solution.py:23
  328.3 21.7 %collective-permute-start.11 = (f32[136,256]{1,0:T(8,128)S(1)}, f32[136,256]{1,0:T(8,128)S(1)}, u32[]{:S(2)}, u32[]{:S(2)}) collective-permute-start(f32[136,256]{1,0:T(8,128)S(1)} %pad_maximum_fusion.4), channel_id=1, source_target_pairs={{0,64},{32,96},{64,128},{96,160},{128,192},{160,224},{192,256},{22... | collective-permute-start | bytes 417800 | tf_op jit(solution)/shard_map/ppermute | solution.py:23
  330.2 24.8 %collective-permute-start.12 = (f32[136,256]{1,0:T(8,128)S(1)}, f32[136,256]{1,0:T(8,128)S(1)}, u32[]{:S(2)}, u32[]{:S(2)}) collective-permute-start(f32[136,256]{1,0:T(8,128)S(1)} %pad_maximum_fusion.4), channel_id=1, source_target_pairs={{0,96},{32,128},{64,160},{96,192},{128,224},{160,256},{192,288},{2... | collective-permute-start | bytes 417800 | tf_op jit(solution)/shard_map/ppermute | solution.py:23
  333.5 41.4 %copy-start.10 = (f32[4,256,256]{1,2,0:T(8,128)S(1)}, f32[4,256,256]{1,2,0:T(8,128)}, u32[]{:S(2)}) copy-start(f32[4,256,256]{1,2,0:T(8,128)} %get-tuple-element.70) | copy-start | bytes 3145732
  333.5 41.4 %copy-start.12 = (bf16[1024,256]{0,1:T(8,128)(2,1)S(1)}, bf16[1024,256]{0,1:T(8,128)(2,1)}, u32[]{:S(2)}) copy-start(bf16[1024,256]{0,1:T(8,128)(2,1)} %fusion.21) | copy-start | bytes 1572868
  355.1 13.2 %collective-permute-start.13 = (f32[136,256]{1,0:T(8,128)S(1)}, f32[136,256]{1,0:T(8,128)S(1)}, u32[]{:S(2)}, u32[]{:S(2)}) collective-permute-start(f32[136,256]{1,0:T(8,128)S(1)} %pad_maximum_fusion.5), channel_id=1, source_target_pairs={{0,32},{32,64},{64,96},{96,128},{128,160},{160,192},{192,224},{224... | collective-permute-start | bytes 417800 | tf_op jit(solution)/shard_map/ppermute | solution.py:23
  357.0 16.5 %collective-permute-start.14 = (f32[136,256]{1,0:T(8,128)S(1)}, f32[136,256]{1,0:T(8,128)S(1)}, u32[]{:S(2)}, u32[]{:S(2)}) collective-permute-start(f32[136,256]{1,0:T(8,128)S(1)} %pad_maximum_fusion.5), channel_id=1, source_target_pairs={{0,160},{32,192},{64,224},{96,256},{128,288},{160,320},{192,352},{... | collective-permute-start | bytes 417800 | tf_op jit(solution)/shard_map/ppermute | solution.py:23
Sparse Core Ops, SparseCore 0:
  175.1 55.0 all-gather.3
